TPU v7x, 32 devices: a whole 2x2x4 slice. The times are simulated.
32 devices in a mesh: groups: 2 (over y), expert: 8 (over z, core), sub: 2 (over x).
Axes of the slice: x: 2, y: 2, z: 4, core: 2. Of those that a mesh axis runs over, the one named last changes fastest.
Arguments:
- latent: bfloat16 [4096, 1024], P(('groups', 'expert', 'sub')), parts along dimension 0, may hold values from -6 to 6
- routes: int32 [4096, 4], P(('groups', 'expert', 'sub')), parts along dimension 0, may hold values from 0 to 7, all different within a row; in each aligned block of 128 rows (0 to 127, 128 to 255, ...) at most 96 rows name the same one
- gates: float32 [4096, 4], P(('groups', 'expert', 'sub')), parts along dimension 0, may hold values from 0.1 to 1
- up_weight: bfloat16 [8, 1024, 2688], P('expert', None, 'sub'), may hold values from -0.1875 to 0.1875
- down_weight: bfloat16 [8, 1024, 2688], P('expert', None, 'sub'), may hold values from -0.125 to 0.125
Outputs:
- mixed: bfloat16 [4096, 1024], P(('groups', 'expert', 'sub')), parts along dimension 0
There are 2 independent parts, one for each index of `groups`. A program takes and returns all parts, laid end to end along the dimension named above; an argument that names none is the same for every part. Nothing has to cross between parts.
Inputs may be any that keep to these rules, and one draw needn't show every extreme that they name: `routes`: each token names 4 different experts; among the 128 tokens of one device no expert is named more than 96 times, a bound that some block reaches.
All inputs are finite; a program needn't handle non-finite values.
Results may differ from a plain program's by a relative error of at most 0.0058.
Values may be sent and summed in bfloat16 or wider, within the bound.
A program may use at most 128 MiB of HBM per device.

v0:
```python
import jax
import jax.numpy as jnp
from jax import lax
from jax.sharding import PartitionSpec as P


def expert_part(row_block, up_part, down_part):
    preact = jnp.dot(row_block, up_part, preferred_element_type=jnp.float32)
    active = jnp.square(jnp.maximum(preact, 0.0)).astype(jnp.bfloat16)
    return lax.dot_general(
        active, down_part, (((1,), (1,)), ((), ())), preferred_element_type=jnp.float32
    )


def local(latent, routes, gates, up_weight, down_weight):
    tokens_here, row_width = latent.shape
    top_count = routes.shape[1]
    experts = lax.axis_size("expert")
    slot_most = min(tokens_here, 3 * tokens_here * top_count // (2 * experts))
    pair_count = tokens_here * top_count
    route_ids = routes.reshape(-1)
    one_hot = (route_ids[:, None] == jnp.arange(experts, dtype=jnp.int32)[None, :]).astype(
        jnp.int32
    )
    before = jnp.cumsum(one_hot, axis=0) - one_hot
    slot_rank = jnp.sum(before * one_hot, axis=1)
    slot_of = route_ids * slot_most + slot_rank
    source = (
        jnp.full((experts * slot_most,), pair_count, jnp.int32)
        .at[slot_of]
        .set(jnp.arange(pair_count, dtype=jnp.int32))
    )
    padded = jnp.concatenate([latent, jnp.zeros((1, row_width), latent.dtype)], axis=0)
    send_rows = padded[source // top_count].reshape(experts, slot_most, row_width)
    arrived = lax.all_to_all(send_rows, "expert", split_axis=0, concat_axis=0, tiled=True)
    flat_rows = arrived.reshape(-1, row_width)
    summed = expert_part(
        flat_rows,
        lax.all_gather(up_weight, "sub", axis=2, tiled=True)[0],
        lax.all_gather(down_weight, "sub", axis=2, tiled=True)[0],
    )
    expert_out = lax.all_to_all(
        summed.astype(jnp.bfloat16).reshape(arrived.shape),
        "expert",
        split_axis=0,
        concat_axis=0,
        tiled=True,
    )
    values = expert_out.reshape(experts * slot_most, row_width)[slot_of].astype(jnp.float32)
    mixed_out = jnp.sum(
        values.reshape(tokens_here, top_count, row_width) * gates[:, :, None], axis=1
    )
    return mixed_out.astype(jnp.bfloat16)


def solution(mesh):
    placed = (
        P(("groups", "expert", "sub"), None),
        P(("groups", "expert", "sub"), None),
        P(("groups", "expert", "sub"), None),
        P("expert", None, "sub"),
        P("expert", None, "sub"),
    )
    return jax.shard_map(
        local,
        mesh=mesh,
        in_specs=placed,
        out_specs=P(("groups", "expert", "sub"), None),
        check_vma=False,
    )
```

profile of v0, /device:TPU:0, one launch (start us, length us, event | category | flops | bytes accessed | tf_op | source)
XLA Modules:
  0.0 220.0 jit_solution(8751266270399759051)
XLA Ops:
  6.5 0.0 copy-start.1
  6.5 0.0 copy-start
  6.5 0.0 all-gather.3.cloned.1.call-start
  6.5 0.7 all-gather.3.cloned.1.call-update
  7.3 0.0 all-gather.5.cloned.1.call-start
  7.3 0.7 all-gather.5.cloned.1.call-update
  8.0 0.0 copy-done.1
  8.0 0.1 copy.8
  8.1 0.1 eq.29
  8.2 0.1 eq.25
  8.4 1.1 reduce-window.6
  9.5 0.2 slice_reduce_fusion
  9.8 0.1 copy.7
  9.9 0.1 mul.29
  10.0 0.0 copy-done
  10.0 0.1 fusion.7
  10.1 2.4 %scatter_custom_fusion = s32[768]{0:T(1024)S(1)} fusion(s32[512]{0:T(512)S(1)} %bitcast.27, s32[512]{0:T(512)S(1)} %iota.11, s32[]{:T(128)} %constant.13.clone.1), kind=kCustom, calls=%fused_computation.27 | custom fusion | bytes 3076 | tf_op jit(solution)/shard_map/scatter | solution.py:31
  12.6 2.8 %gather_fusion = bf16[768,1024]{1,0:T(8,128)(2,1)S(1)} fusion(bf16[129,1024]{1,0:T(8,128)(2,1)S(1)} %concatenate.3, s32[1024]{0:T(1024)S(1)} %pad_clamp_fusion.1), kind=kCustom, calls=%fused_computation | custom fusion | bytes 3148800 | tf_op jit(solution)/shard_map/gather | solution.py:34
  15.5 43.9 %all_to_all.10 = bf16[8,96,1024]{2,1,0:T(8,128)(2,1)S(1)} all-to-all(bf16[8,96,1024]{2,1,0:T(8,128)(2,1)S(1)} %bitcast.25), channel_id=1, replica_groups=mesh['groups'=2,'expert'=8,'sub'=2] {'expert'}, dimensions={0} | all-to-all | bytes 3145728 | tf_op jit(solution)/shard_map/all_to_all | solution.py:35
  59.4 23.7 %all-gather.3.cloned.1.call-done = bf16[1,1024,2688]{1,2,0:T(8,128)(2,1)} async-done(((bf16[1,1024,1344]{1,2,0:T(8,128)(2,1)}), bf16[1,1024,2688]{1,2,0:T(8,128)(2,1)}) %all-gather.3.cloned.1.call-update) | async-done | bytes 5505040 | tf_op jit(solution)/shard_map/all_gather | solution.py:39
  83.1 8.8 %multiply_convert_fusion = bf16[768,2688]{1,0:T(8,128)(2,1)} fusion(bf16[768,1024]{1,0:T(8,128)(2,1)S(1)} %bitcast.26, bf16[1,1024,2688]{1,2,0:T(8,128)(2,1)} %all-gather.3.cloned.1.call-done), kind=kOutput, calls=%fused_computation.3 | convolution fusion | flops 4234051584 | bytes 11206656 | tf_op jit(solution)/shard_map/dot_general | solution.py:8
  91.9 64.3 %all-gather.5.cloned.1.call-done = bf16[1,1024,2688]{1,2,0:T(8,128)(2,1)} async-done(((bf16[1,1024,1344]{1,2,0:T(8,128)(2,1)}), bf16[1,1024,2688]{1,2,0:T(8,128)(2,1)}) %all-gather.5.cloned.1.call-update) | async-done | bytes 5505040 | tf_op jit(solution)/shard_map/all_gather | solution.py:40
  156.2 9.6 %fusion.3 = bf16[768,1024]{1,0:T(8,128)(2,1)} fusion(bf16[768,2688]{1,0:T(8,128)(2,1)} %multiply_convert_fusion, bf16[1,1024,2688]{1,2,0:T(8,128)(2,1)} %all-gather.5.cloned.1.call-done), kind=kOutput, calls=%fused_computation.8 | convolution fusion | flops 4228644864 | bytes 11206656 | tf_op jit(solution)/shard_map/dot_general | solution.py:10
  165.8 0.0 copy-start.2
  165.8 4.7 %all-to-all-start.1 = ((bf16[8,96,1024]{2,1,0:T(8,128)(2,1)}), bf16[8,96,1024]{2,1,0:T(8,128)(2,1)S(1)}, u32[]{:S(2)}, u32[]{:S(2)}) async-start(bf16[8,96,1024]{2,1,0:T(8,128)(2,1)} %bitcast.8), calls=%async_computation.1 | async-start | bytes 3145728 | tf_op jit(solution)/shard_map/all_to_all | solution.py:42
  170.6 0.0 copy-done.2
  170.6 0.1 copy.10
  170.7 37.7 %all-to-all-done.1 = bf16[8,96,1024]{2,1,0:T(8,128)(2,1)S(1)} async-done(((bf16[8,96,1024]{2,1,0:T(8,128)(2,1)}), bf16[8,96,1024]{2,1,0:T(8,128)(2,1)S(1)}, u32[]{:S(2)}, u32[]{:S(2)}) %all-to-all-start.1) | async-done | bytes 1572896 | tf_op jit(solution)/shard_map/all_to_all | solution.py:42
  208.4 2.0 gather_fusion.1
  210.4 0.7 reshape.68
  211.1 2.1 multiply_reduce_fusion
  (10 shorter events, 0.1 us)
Async XLA Ops:
  6.5 1.5 copy-start.1
  6.5 3.5 %copy-start = (bf16[128,1024]{1,0:T(8,128)(2,1)S(1)}, bf16[128,1024]{1,0:T(8,128)(2,1)}, u32[]{:S(2)}) copy-start(bf16[128,1024]{1,0:T(8,128)(2,1)} %param.5) | copy-start | bytes 786436
  6.5 76.6 %all-gather.3.cloned.1.call-start = ((), (), s32[]{:S(2)}) async-start(), calls=%async_computation.2 | async-start | bytes 8257536 | tf_op jit(solution)/shard_map/all_gather | solution.py:39
  7.3 149.0 %all-gather.5.cloned.1.call-start = ((), (), s32[]{:S(2)}) async-start(), calls=%async_computation.3 | async-start | bytes 8257536 | tf_op jit(solution)/shard_map/all_gather | solution.py:40
  165.8 4.7 %copy-start.2 = (f32[128,4]{0,1:T(4,128)S(1)}, f32[128,4]{0,1:T(4,128)}, u32[]{:S(2)}) copy-start(f32[128,4]{0,1:T(4,128)} %param.7) | copy-start | bytes 6148
  165.8 42.5 %all-to-all-start.1 = ((bf16[8,96,1024]{2,1,0:T(8,128)(2,1)}), bf16[8,96,1024]{2,1,0:T(8,128)(2,1)S(1)}, u32[]{:S(2)}, u32[]{:S(2)}) async-start(bf16[8,96,1024]{2,1,0:T(8,128)(2,1)} %bitcast.8), calls=%async_computation.1 | async-start | bytes 3145728 | tf_op jit(solution)/shard_map/all_to_all | solution.py:42
Sparse Core Ops, SparseCore 0:
  8.9 74.2 all-gather.2
  84.7 71.4 all-gather.4
where the time goes:
time: 220 us
  waiting for transfers between devices  127 us (58%)
  blocking collectives  43.9 us (20%)
  matrix products  18.4 us (8%)
  between operations  13.5 us (6%)
  local copies, waits for them, and re-layouts  8.93 us (4%)
  starting transfers between devices  4.78 us (2%)
  other arithmetic  3.39 us (2%)
    all_gather x1, waiting for transfers between devices, local(): lax.all_gather(down_weight, 'sub', axis=2, tiled=True)[0]  64.3 us
    all_to_all x1, blocking collectives, local(): lax.all_to_all(send_rows, 'expert', split_axis=0, concat_axis=0, tiled=True)  43.9 us
    all_to_all x1, waiting for transfers between devices, local(): lax.all_to_all(summed.astype(jnp.bfloat16).reshape(arrived.shape), 'exper...  37.7 us
    all_gather x1, waiting for transfers between devices, local(): lax.all_gather(up_weight, 'sub', axis=2, tiled=True)[0]  23.7 us
    dot_general x1, matrix products, expert_part(): lax.dot_general(active, down_part, (((1,), (1,)), ((), ())), preferred_el...  9.62 us
    dot_general x1, matrix products, expert_part(): preact = jnp.dot(row_block, up_part, preferred_element_type=jnp.float32)  8.77 us
    all_to_all x1, starting transfers between devices, local(): lax.all_to_all(summed.astype(jnp.bfloat16).reshape(arrived.shape), 'exper...  4.74 us
  transfers between devices with their start and end apart: 3, of which 3 were waited for; matrix products, arithmetic and copies ran while one was open for 7% of the time, Pallas kernels for 0%

commit v1 on v0

--- a/solution.py
+++ b/solution.py
@@ -36,7 +36,9 @@
     flat_rows = arrived.reshape(-1, row_width)
     summed = expert_part(
         flat_rows,
-        lax.all_gather(up_weight, "sub", axis=2, tiled=True)[0],
+        jnp.concatenate(
+            lax.all_to_all(jnp.stack([up_weight] * lax.axis_size("sub")), "sub", 0, 0), axis=2
+        )[0],
         lax.all_gather(down_weight, "sub", axis=2, tiled=True)[0],
     )
     expert_out = lax.all_to_all(

time: 220 us -> 230 us (1.045)
  waiting for transfers between devices: 127 us -> 72.6 us
  blocking collectives: 43.9 us -> 96.2 us
  starting transfers between devices: 4.78 us -> 11.3 us
  other arithmetic: 3.39 us -> 6.98 us
  local copies, waits for them, and re-layouts: 8.93 us -> 11.3 us
    all_gather x1, waiting for transfers between devices: 64.3 us -> 0.01 us  [local(): lax.all_gather(down_weight, 'sub', axis=2, tiled=True)[0]]
    all_to_all x1, blocking collectives: 43.9 us -> 96.2 us  [local(): lax.all_to_all(jnp.stack([up_weight] * lax.axis_size('sub')), 'sub', 0, 0)]
    all_to_all x0 -> x1, waiting for transfers between devices: none -> 34.2 us  [local(): lax.all_to_all(send_rows, 'expert', split_axis=0, concat_axis=0, tiled=True)]
    all_gather x1 -> x0, waiting for transfers between devices: 23.7 us -> none  [local(): lax.all_gather(up_weight, 'sub', axis=2, tiled=True)[0]]
    all_to_all x0 -> x1, starting transfers between devices: none -> 6.62 us  [local(): lax.all_to_all(send_rows, 'expert', split_axis=0, concat_axis=0, tiled=True)]
    another operation x2 -> x3, other arithmetic: 1.18 us -> 4.09 us  [the longest x1 2.93 us: local(): jnp.stack([up_weight] * lax.axis_size('sub'))]
  transfers between devices with their start and end apart: 3 -> 3, of which waited for: 3 -> 2; matrix products, arithmetic and copies ran while one was open for 7% -> 5% of each run, Pallas kernels for 0% -> 0%
where the time goes in v1:
time: 230 us; the launch traced here: 229 us
  blocking collectives  96.2 us (42%)
  waiting for transfers between devices  72.6 us (32%)
  matrix products  17.7 us (8%)
  between operations  13.5 us (6%)
  local copies, waits for them, and re-layouts  11.3 us (5%)
  starting transfers between devices  11.3 us (5%)
  other arithmetic  6.98 us (3%)
    all_to_all x1, blocking collectives, local(): lax.all_to_all(jnp.stack([up_weight] * lax.axis_size('sub')), 'sub', 0, 0)  96.2 us
    all_to_all x1, waiting for transfers between devices, local(): lax.all_to_all(summed.astype(jnp.bfloat16).reshape(arrived.shape), 'exper...  37.7 us
    all_to_all x1, waiting for transfers between devices, local(): lax.all_to_all(send_rows, 'expert', split_axis=0, concat_axis=0, tiled=True)  34.2 us
    dot_general x1, matrix products, expert_part(): lax.dot_general(active, down_part, (((1,), (1,)), ((), ())), preferred_el...  9.6 us
    dot_general x1, matrix products, expert_part(): preact = jnp.dot(row_block, up_part, preferred_element_type=jnp.float32)  8.13 us
    all_to_all x1, starting transfers between devices, local(): lax.all_to_all(send_rows, 'expert', split_axis=0, concat_axis=0, tiled=True)  6.62 us
    all_to_all x1, starting transfers between devices, local(): lax.all_to_all(summed.astype(jnp.bfloat16).reshape(arrived.shape), 'exper...  4.6 us
  transfers between devices with their start and end apart: 3, of which 2 were waited for; matrix products, arithmetic and copies ran while one was open for 5% of the time, Pallas kernels for 0%

profile of v1, /device:TPU:0, one launch (start us, length us, event | category | flops | bytes accessed | tf_op | source)
XLA Modules:
  0.0 229.5 jit_solution(6000950186432391372)
XLA Ops:
  6.5 0.8 copy.8
  7.3 0.1 eq.29
  7.4 0.1 eq.25
  7.5 0.7 broadcast_multiply_fusion
  8.2 1.1 reduce-window.6
  9.4 0.2 slice_reduce_fusion
  9.6 0.1 copy.7
  9.7 0.1 mul.29
  9.8 0.1 fusion.6
  10.0 2.4 %scatter_custom_fusion = s32[768]{0:T(1024)S(1)} fusion(s32[512]{0:T(512)S(1)} %bitcast.29, s32[512]{0:T(512)S(1)} %iota.11, s32[]{:T(128)} %constant.13.clone.1), kind=kCustom, calls=%fused_computation.27 | custom fusion | bytes 3076 | tf_op jit(solution)/shard_map/scatter | solution.py:31
  12.4 1.0 concatenate.3
  13.4 3.6 %gather_fusion = bf16[768,1024]{1,0:T(8,128)(2,1)} fusion(bf16[129,1024]{1,0:T(8,128)(2,1)S(1)} %concatenate.3, s32[1024]{0:T(1024)S(1)} %pad_clamp_fusion.1), kind=kCustom, calls=%fused_computation | custom fusion | bytes 3148800 | tf_op jit(solution)/shard_map/gather | solution.py:34
  17.0 0.0 copy-start
  17.0 6.6 %all-to-all-start = ((bf16[8,96,1024]{2,1,0:T(8,128)(2,1)}), bf16[8,96,1024]{2,1,0:T(8,128)(2,1)}, u32[]{:S(2)}, u32[]{:S(2)}) async-start(bf16[8,96,1024]{2,1,0:T(8,128)(2,1)} %bitcast.4), calls=%async_computation | async-start | bytes 3145728 | tf_op jit(solution)/shard_map/all_to_all | solution.py:35
  23.6 0.0 all-gather.2.cloned.1.call-start
  23.7 0.7 all-gather.2.cloned.1.call-update
  24.3 0.0 copy-done
  24.4 2.9 %pad_maximum_fusion = bf16[2,1,1024,1344]{2,3,1,0:T(8,128)(2,1)} fusion(bf16[1,1,1024,1344]{2,3,1,0:T(8,128)(2,1)S(1)} %bitcast.28), kind=kLoop, calls=%fused_computation.4 | loop fusion | flops 2752512 | bytes 8257536 | tf_op jit(solution)/shard_map/stack | solution.py:40
  27.3 34.2 %all-to-all-done = bf16[8,96,1024]{2,1,0:T(8,128)(2,1)} async-done(((bf16[8,96,1024]{2,1,0:T(8,128)(2,1)}), bf16[8,96,1024]{2,1,0:T(8,128)(2,1)}, u32[]{:S(2)}, u32[]{:S(2)}) %all-to-all-start) | async-done | bytes 1572896 | tf_op jit(solution)/shard_map/all_to_all | solution.py:35
  61.5 96.2 %all_to_all.15 = bf16[2,1,1024,1344]{2,3,1,0:T(8,128)(2,1)S(1)} all-to-all(bf16[2,1,1024,1344]{2,3,1,0:T(8,128)(2,1)} %pad_maximum_fusion), channel_id=1, replica_groups=mesh['groups'=2,'expert'=8,'sub'=2] {'sub'}, dimensions={0} | all-to-all | bytes 11010048 | tf_op jit(solution)/shard_map/all_to_all | solution.py:40
  157.7 8.1 %multiply_convert_fusion = bf16[768,2688]{1,0:T(8,128)(2,1)} fusion(bf16[768,1024]{1,0:T(8,128)(2,1)} %bitcast.5, bf16[1024,2688]{0,1:T(8,128)(2,1)S(1)} %bitcast.27), kind=kOutput, calls=%fused_computation.3 | convolution fusion | flops 4234051584 | bytes 11206656 | tf_op jit(solution)/shard_map/dot_general | solution.py:8
  165.8 0.0 copy-start.1
  165.8 0.0 all-gather.2.cloned.1.call-done
  165.8 9.6 %fusion.2 = bf16[768,1024]{1,0:T(8,128)(2,1)} fusion(bf16[768,2688]{1,0:T(8,128)(2,1)} %multiply_convert_fusion, bf16[1,1024,2688]{1,2,0:T(8,128)(2,1)} %all-gather.2.cloned.1.call-done), kind=kOutput, calls=%fused_computation.8 | convolution fusion | flops 4228644864 | bytes 11206656 | tf_op jit(solution)/shard_map/dot_general | solution.py:10
  175.4 4.6 %all-to-all-start.2 = ((bf16[8,96,1024]{2,1,0:T(8,128)(2,1)}), bf16[8,96,1024]{2,1,0:T(8,128)(2,1)S(1)}, u32[]{:S(2)}, u32[]{:S(2)}) async-start(bf16[8,96,1024]{2,1,0:T(8,128)(2,1)} %bitcast.10), calls=%async_computation.2 | async-start | bytes 3145728 | tf_op jit(solution)/shard_map/all_to_all | solution.py:44
  180.0 0.0 copy-done.1
  180.0 0.1 copy.10
  180.1 37.7 %all-to-all-done.2 = bf16[8,96,1024]{2,1,0:T(8,128)(2,1)S(1)} async-done(((bf16[8,96,1024]{2,1,0:T(8,128)(2,1)}), bf16[8,96,1024]{2,1,0:T(8,128)(2,1)S(1)}, u32[]{:S(2)}, u32[]{:S(2)}) %all-to-all-start.2) | async-done | bytes 1572896 | tf_op jit(solution)/shard_map/all_to_all | solution.py:44
  217.8 2.0 gather_fusion.1
  219.9 0.7 reshape.72
  220.6 2.1 multiply_reduce_fusion
  (8 shorter events, 0.1 us)
Async XLA Ops:
  17.0 7.4 %copy-start = (bf16[1,1024,1344]{1,2,0:T(8,128)(2,1)S(1)}, bf16[1,1024,1344]{1,2,0:T(8,128)(2,1)}, u32[]{:S(2)}) copy-start(bf16[1,1024,1344]{1,2,0:T(8,128)(2,1)} %param.8) | copy-start | bytes 8257540
  17.0 44.5 %all-to-all-start = ((bf16[8,96,1024]{2,1,0:T(8,128)(2,1)}), bf16[8,96,1024]{2,1,0:T(8,128)(2,1)}, u32[]{:S(2)}, u32[]{:S(2)}) async-start(bf16[8,96,1024]{2,1,0:T(8,128)(2,1)} %bitcast.4), calls=%async_computation | async-start | bytes 3145728 | tf_op jit(solution)/shard_map/all_to_all | solution.py:35
  23.6 142.2 %all-gather.2.cloned.1.call-start = ((), (), s32[]{:S(2)}) async-start(), calls=%async_computation.3 | async-start | bytes 8257536 | tf_op jit(solution)/shard_map/all_gather | solution.py:42
  165.8 14.2 %copy-start.1 = (f32[128,4]{0,1:T(4,128)S(1)}, f32[128,4]{0,1:T(4,128)}, u32[]{:S(2)}) copy-start(f32[128,4]{0,1:T(4,128)} %param.7) | copy-start | bytes 6148
  175.4 42.4 %all-to-all-start.2 = ((bf16[8,96,1024]{2,1,0:T(8,128)(2,1)}), bf16[8,96,1024]{2,1,0:T(8,128)(2,1)S(1)}, u32[]{:S(2)}, u32[]{:S(2)}) async-start(bf16[8,96,1024]{2,1,0:T(8,128)(2,1)} %bitcast.10), calls=%async_computation.2 | async-start | bytes 3145728 | tf_op jit(solution)/shard_map/all_to_all | solution.py:44
Sparse Core Ops, SparseCore 0:
  26.0 103.2 all-gather.1
